TPU v7x, 256 devices: a whole 4x4x8 slice. The times are simulated.
256 devices in a mesh: group: 8 (over z), row: 32 (over y, x, core).
Axes of the slice: x: 4, y: 4, z: 8, core: 2. Of those that a mesh axis runs over, the one named last changes fastest.
Arguments:
- start_basis: float32 [2048, 16, 128], P(('group', 'row')), may hold values from -6 to 6
- tiles: bfloat16 [2048, 16, 128, 128], P(('group', 'row')), may hold values from -60000 to 60000
- tile_cols: int32 [2048, 16], P(('group', 'row')), may hold values from 0 to 75, as said below
- tile_count: int32 [2048], P(('group', 'row')), may hold values from 10 to 16, as said below
- recv_list: int32 [8, 32, 32, 2], P('group', 'row'), may hold values from -1 to 2047, as said below
Outputs:
- krylov: float32 [3, 2048, 16, 128], P(None, ('group', 'row'))
Inputs may be any that keep to these rules, and one draw needn't show every extreme that they name: For each reader device and each other device of its range, recv_list names distinct blocks of that peer in its first slots and -1 in the rest; a reader's own entry is all -1; every reader gets exactly 2 blocks from some peer. tile_cols never names an empty receive slot, nor a rim slot of a range that does not exist (before the first or after the last group); every filled receive slot and every existing rim slot is named by some tile slot below 10. `tile_count`: every device has a row block with all 16 tiles live.
All inputs are finite; a program needn't handle non-finite values.
Results may differ from a plain program's by a relative error of at most 0.0003.
Values sent between devices are 32-bit elements; how exact they have to be, the bound alone decides.
A program may use at most 64 MiB of HBM per device.

v0:
```python
import jax
import jax.numpy as jnp
from jax import lax
from jax.sharding import PartitionSpec as P

SLOTS = 2
RIM = 2
ITERS = 3


def padded(x, sides, width):
    for axis, dim in sides:
        count, length = (lax.axis_size(axis), x.shape[dim])
        up = [(i, (i + 1) % count) for i in range(count - 1)]
        down = [(j, i) for i, j in up]
        last = lax.slice_in_dim(x, length - width, length, axis=dim)
        leading = lax.slice_in_dim(x, 0, width, axis=dim)
        before = lax.ppermute(last, axis, up)
        after = lax.ppermute(leading, axis, down)
        x = jnp.concatenate([before, x, after], axis=dim)
    return x


def orthonormal(applied, gram_sum, row_total):
    vectors = applied.shape[1]
    factor = jnp.linalg.cholesky(gram_sum / row_total)
    inverse = lax.linalg.triangular_solve(
        factor, jnp.eye(vectors, dtype=jnp.float32), left_side=True, lower=True
    )
    return jnp.einsum("kl,bli->bki", inverse, applied, precision=lax.Precision.HIGHEST)


def local(start_basis, tiles, tile_cols, tile_count, recv_list):
    groups = lax.axis_size("group")
    peers = lax.axis_size("row")
    group_at = lax.axis_index("group")
    blocks = tiles.shape[0]
    per_row = tiles.shape[1]
    tile_side = tiles.shape[2]
    row_total = groups * peers * blocks * tile_side
    live_mask = (jnp.arange(per_row, dtype=jnp.int32)[None, :] < tile_count[:, None]).astype(
        jnp.float32
    )
    wide_tiles = tiles.astype(jnp.float32)
    sum_sq = jnp.einsum(
        "btij,bt->bi", wide_tiles * wide_tiles, live_mask, precision=lax.Precision.HIGHEST
    )
    inv_root = (1e-06 + sum_sq) ** (-0.25)
    wanted = recv_list.reshape(peers, SLOTS)
    gather_pick = jnp.clip(wanted - group_at * peers * blocks, 0, peers * blocks - 1).reshape(-1)
    results = []
    basis = start_basis
    for step_at in range(ITERS):
        scaled = basis * inv_root[:, None, :]
        rimmed = padded(scaled, (("group", 0),), RIM)
        group_all = lax.all_gather(scaled, "row", axis=0, tiled=True)
        received = jnp.take(group_all, gather_pick, axis=0)
        extended = jnp.concatenate([scaled, received, rimmed[:RIM], rimmed[blocks + RIM :]], axis=0)
        picked = jnp.take(extended, tile_cols, axis=0) * live_mask[:, :, None, None]
        product = jnp.einsum(
            "btij,btkj->bki",
            tiles,
            picked,
            precision=lax.Precision.HIGHEST,
            preferred_element_type=jnp.float32,
        )
        applied = product * inv_root[:, None, :]
        partial_value = jnp.einsum("bki,bli->kl", applied, applied, precision=lax.Precision.HIGHEST)
        gram_sum = lax.psum(partial_value, ("group", "row"))
        basis = orthonormal(applied, gram_sum, row_total)
        results.append(basis)
    return jnp.stack(results)


def solution(mesh):
    placed = (
        P(("group", "row"), None, None),
        P(("group", "row"), None, None, None),
        P(("group", "row"), None),
        P(("group", "row")),
        P("group", "row", None, None),
    )
    return jax.shard_map(
        local,
        mesh=mesh,
        in_specs=placed,
        out_specs=P(None, ("group", "row"), None, None),
        check_vma=False,
    )
```

profile of v0, /device:TPU:1, one launch (start us, length us, event | category | flops | bytes accessed | tf_op | source)
XLA Modules:
  0.0 434.7 jit_solution(10057653734697218750)
XLA Ops:
  6.6 4.5 %multiply_reduce_fusion = f32[8,16,128]{2,1,0:T(8,128)S(1)} fusion(bf16[8,16,128,128]{3,2,1,0:T(8,128)(2,1)} %param.13), kind=kLoop, calls=%fused_computation.6 | loop fusion | flops 6275072 | bytes 4259840 | tf_op jit(solution)/shard_map/btij,bt->bi/reduce_sum | solution.py:45
  11.1 0.1 fusion.26
  11.1 0.2 fusion.12
  11.3 0.6 broadcast_multiply_fusion
  12.0 0.0 all-gather.6.cloned.1.call-start
  12.0 0.7 fusion.33
  12.8 4.4 %collective-permute-start = (f32[2,16,128]{2,1,0:T(8,128)S(1)}, f32[2,16,128]{2,1,0:T(8,128)S(1)}, u32[]{:S(2)}, u32[]{:S(2)}) collective-permute-start(f32[2,16,128]{2,1,0:T(8,128)S(1)} %get-tuple-element.13), channel_id=1, source_target_pairs={{0,32},{32,64},{64,96},{96,128},{128,160},{160,192},{192,224},{1,3... | collective-permute-start | bytes 49160 | tf_op jit(solution)/shard_map/ppermute | solution.py:18
  17.2 1.3 collective-permute-start.1
  18.5 0.1 reshape.114
  18.6 0.1 copy.20
  18.6 0.1 min.12
  18.8 46.4 %all-gather.4.cloned.1.call-done = f32[256,16,128]{2,1,0:T(8,128)} async-done(((f32[8,16,128]{2,1,0:T(8,128)}), f32[256,16,128]{2,1,0:T(8,128)}) %all-gather.4.cloned.1.call-update) | async-done | bytes 2097168 | tf_op jit(solution)/shard_map/all_gather | solution.py:56
  65.2 2.2 gather_fusion
  67.4 0.1 broadcast_select_fusion.2
  67.6 0.9 pad_maximum_fusion
  68.5 0.8 gather_fusion.1
  69.2 5.2 %fusion.2 = f32[8,16,128]{2,1,0:T(8,128)S(1)} fusion(bf16[8,16,128,128]{3,2,1,0:T(8,128)(2,1)} %param.13, f32[8,16,16,128]{3,2,1,0:T(8,128)S(1)} %bitcast.92, f32[8,16]{1,0:T(8,128)S(1)} %get-tuple-element.15, pred[8,16]{1,0:T(8,128)(4,1)S(1)} %get-tuple-element.21, f32[8,128]{1,0:T(8,128)S(1)} %add_power_fusion), kind=kOutput, calls=%fused_computation.13 | convolution fusion | flops 403193856 | bytes 5313152 | tf_op jit(solution)/shard_map/btij,btkj->bki/dot_general | solution.py:60
  74.4 0.2 convolution_bitcast_fusion.9
  74.6 75.6 %psum.21 = f32[16,16]{0,1:T(8,128)S(1)} all-reduce(f32[16,16]{0,1:T(8,128)S(1)} %convolution_bitcast_fusion.9), channel_id=1, replica_groups=mesh['group'=8,'row'=32] {'group','row'}, use_global_device_ids=true, to_apply=%region_1.0 | all-reduce | flops 256 | bytes 2048 | tf_op jit(solution)/shard_map/psum | solution.py:69
  150.2 0.1 copy.22
  150.3 1.5 cholesky.59
  151.7 0.6 compare_reduce_fusion.2
  152.4 0.6 fusion.17
  153.0 1.2 custom-call.7
  154.3 0.2 convolution_bitcast_fusion.8
  154.5 0.8 bitcast_multiply_fusion.1
  155.3 0.0 all-gather.8.cloned.1.call-start
  155.4 0.7 fusion.32
  156.1 2.9 collective-permute-start.2
  159.1 1.3 collective-permute-start.3
  160.4 41.2 %all-gather.6.cloned.1.call-done = f32[256,16,128]{2,1,0:T(8,128)} async-done(((f32[8,16,128]{2,1,0:T(8,128)}), f32[256,16,128]{2,1,0:T(8,128)}) %all-gather.6.cloned.1.call-update) | async-done | bytes 2097168 | tf_op jit(solution)/shard_map/all_gather | solution.py:56
  201.6 2.2 gather_fusion.2
  203.8 0.1 broadcast_select_fusion.1
  204.0 0.9 pad_maximum_fusion.1
  204.9 0.8 gather_fusion.3
  205.6 5.2 %fusion.1 = f32[8,16,128]{2,1,0:T(8,128)S(1)} fusion(bf16[8,16,128,128]{3,2,1,0:T(8,128)(2,1)} %param.13, f32[8,16,16,128]{3,2,1,0:T(8,128)S(1)} %bitcast.93, f32[8,16]{1,0:T(8,128)S(1)} %get-tuple-element.15, pred[8,16]{1,0:T(8,128)(4,1)S(1)} %get-tuple-element.21, f32[8,128]{1,0:T(8,128)S(1)} %add_power_fusion), kind=kOutput, calls=%fused_computation.11 | convolution fusion | flops 403193856 | bytes 5313152 | tf_op jit(solution)/shard_map/btij,btkj->bki/dot_general | solution.py:60
  210.8 0.2 convolution_bitcast_fusion.7
  211.0 75.6 %psum.22 = f32[16,16]{0,1:T(8,128)S(1)} all-reduce(f32[16,16]{0,1:T(8,128)S(1)} %convolution_bitcast_fusion.7), channel_id=1, replica_groups=mesh['group'=8,'row'=32] {'group','row'}, use_global_device_ids=true, to_apply=%region_4.9 | all-reduce | flops 256 | bytes 2048 | tf_op jit(solution)/shard_map/psum | solution.py:69
  286.6 0.1 copy.24
  286.6 1.5 cholesky.70
  288.1 0.6 compare_reduce_fusion.1
  288.8 0.6 fusion.18
  289.4 1.2 custom-call.8
  290.7 0.2 convolution_bitcast_fusion.6
  290.9 0.8 bitcast_multiply_fusion
  291.7 0.7 fusion.31
  292.5 2.9 collective-permute-start.4
  295.4 1.3 collective-permute-start.5
  296.7 41.3 %all-gather.8.cloned.1.call-done = f32[256,16,128]{2,1,0:T(8,128)} async-done(((f32[8,16,128]{2,1,0:T(8,128)}), f32[256,16,128]{2,1,0:T(8,128)}) %all-gather.8.cloned.1.call-update) | async-done | bytes 2097168 | tf_op jit(solution)/shard_map/all_gather | solution.py:56
  338.0 2.2 gather_fusion.4
  340.2 0.1 broadcast_select_fusion
  340.4 0.9 pad_maximum_fusion.2
  341.2 0.8 gather_fusion.5
  342.0 5.2 %fusion = f32[8,16,128]{2,1,0:T(8,128)S(1)} fusion(bf16[8,16,128,128]{3,2,1,0:T(8,128)(2,1)} %param.13, f32[8,16,16,128]{3,2,1,0:T(8,128)S(1)} %bitcast.91, f32[8,16]{1,0:T(8,128)S(1)} %get-tuple-element.15, pred[8,16]{1,0:T(8,128)(4,1)S(1)} %get-tuple-element.21, f32[8,128]{1,0:T(8,128)S(1)} %add_power_fusion), kind=kOutput, calls=%fused_computation.9 | convolution fusion | flops 403193856 | bytes 5313152 | tf_op jit(solution)/shard_map/btij,btkj->bki/dot_general | solution.py:60
  347.2 0.2 convolution_bitcast_fusion.5
  347.4 75.6 %psum.23 = f32[16,16]{0,1:T(8,128)S(1)} all-reduce(f32[16,16]{0,1:T(8,128)S(1)} %convolution_bitcast_fusion.5), channel_id=1, replica_groups=mesh['group'=8,'row'=32] {'group','row'}, use_global_device_ids=true, to_apply=%region_5.10 | all-reduce | flops 256 | bytes 2048 | tf_op jit(solution)/shard_map/psum | solution.py:69
  422.9 0.1 copy.26
  423.0 1.5 cholesky.81
  424.5 0.6 compare_reduce_fusion
  425.2 0.6 fusion.19
  425.8 1.2 custom-call.9
  427.0 0.2 convolution_bitcast_fusion.4
  427.2 0.2 convolution_bitcast_fusion
  427.5 0.7 pad_maximum_fusion.3
  (34 shorter events, 0.3 us)
Async XLA Ops:
  6.5 4.5 %copy-start.1 = (s32[8,16]{1,0:T(8,128)S(1)}, s32[8,16]{1,0:T(8,128)}, u32[]{:S(2)}) copy-start(s32[8,16]{1,0:T(8,128)} %param.14) | copy-start | bytes 1540
  6.5 4.5 %copy-start.3 = (s32[8]{0:T(128)S(1)}, s32[8]{0:T(128)}, u32[]{:S(2)}) copy-start(s32[8]{0:T(128)} %param.15) | copy-start | bytes 100
  6.5 4.8 %copy-start = (f32[8,16,128]{2,1,0:T(8,128)S(1)}, f32[8,16,128]{2,1,0:T(8,128)}, u32[]{:S(2)}) copy-start(f32[8,16,128]{2,1,0:T(8,128)} %param.12) | copy-start | bytes 196612
  6.5 12.0 %copy-start.2 = (s32[1,1,32,2]{2,3,1,0:T(2,128)S(1)}, s32[1,1,32,2]{2,3,1,0:T(2,128)}, u32[]{:S(2)}) copy-start(s32[1,1,32,2]{2,3,1,0:T(2,128)} %param.16) | copy-start | bytes 772
  6.5 58.7 %all-gather.4.cloned.1.call-start = ((), (), s32[]{:S(2)}) async-start(), calls=%async_computation | async-start | bytes 2162688 | tf_op jit(solution)/shard_map/all_gather | solution.py:56
  12.0 189.6 %all-gather.6.cloned.1.call-start = ((), (), s32[]{:S(2)}) async-start(), calls=%async_computation.1 | async-start | bytes 2162688 | tf_op jit(solution)/shard_map/all_gather | solution.py:56
  12.8 54.8 %collective-permute-start = (f32[2,16,128]{2,1,0:T(8,128)S(1)}, f32[2,16,128]{2,1,0:T(8,128)S(1)}, u32[]{:S(2)}, u32[]{:S(2)}) collective-permute-start(f32[2,16,128]{2,1,0:T(8,128)S(1)} %get-tuple-element.13), channel_id=1, source_target_pairs={{0,32},{32,64},{64,96},{96,128},{128,160},{160,192},{192,224},{1,3... | collective-permute-start | bytes 49160 | tf_op jit(solution)/shard_map/ppermute | solution.py:18
  17.2 50.4 %collective-permute-start.1 = (f32[2,16,128]{2,1,0:T(8,128)S(1)}, f32[2,16,128]{2,1,0:T(8,128)S(1)}, u32[]{:S(2)}, u32[]{:S(2)}) collective-permute-start(f32[2,16,128]{2,1,0:T(8,128)S(1)} %get-tuple-element.14), channel_id=1, source_target_pairs={{32,0},{64,32},{96,64},{128,96},{160,128},{192,160},{224,192},{33,... | collective-permute-start | bytes 49160 | tf_op jit(solution)/shard_map/ppermute | solution.py:19
  155.3 182.7 %all-gather.8.cloned.1.call-start = ((), (), s32[]{:S(2)}) async-start(), calls=%async_computation.2 | async-start | bytes 2162688 | tf_op jit(solution)/shard_map/all_gather | solution.py:56
  156.1 47.8 %collective-permute-start.2 = (f32[2,16,128]{2,1,0:T(8,128)S(1)}, f32[2,16,128]{2,1,0:T(8,128)S(1)}, u32[]{:S(2)}, u32[]{:S(2)}) collective-permute-start(f32[2,16,128]{2,1,0:T(8,128)S(1)} %get-tuple-element.10), channel_id=1, source_target_pairs={{0,32},{32,64},{64,96},{96,128},{128,160},{160,192},{192,224},{1,3... | collective-permute-start | bytes 49160 | tf_op jit(solution)/shard_map/ppermute | solution.py:18
  159.1 44.9 %collective-permute-start.3 = (f32[2,16,128]{2,1,0:T(8,128)S(1)}, f32[2,16,128]{2,1,0:T(8,128)S(1)}, u32[]{:S(2)}, u32[]{:S(2)}) collective-permute-start(f32[2,16,128]{2,1,0:T(8,128)S(1)} %get-tuple-element.12), channel_id=1, source_target_pairs={{32,0},{64,32},{96,64},{128,96},{160,128},{192,160},{224,192},{33,... | collective-permute-start | bytes 49160 | tf_op jit(solution)/shard_map/ppermute | solution.py:19
  292.5 47.9 %collective-permute-start.4 = (f32[2,16,128]{2,1,0:T(8,128)S(1)}, f32[2,16,128]{2,1,0:T(8,128)S(1)}, u32[]{:S(2)}, u32[]{:S(2)}) collective-permute-start(f32[2,16,128]{2,1,0:T(8,128)S(1)} %get-tuple-element.6), channel_id=1, source_target_pairs={{0,32},{32,64},{64,96},{96,128},{128,160},{160,192},{192,224},{1,3... | collective-permute-start | bytes 49160 | tf_op jit(solution)/shard_map/ppermute | solution.py:18
  295.4 44.9 %collective-permute-start.5 = (f32[2,16,128]{2,1,0:T(8,128)S(1)}, f32[2,16,128]{2,1,0:T(8,128)S(1)}, u32[]{:S(2)}, u32[]{:S(2)}) collective-permute-start(f32[2,16,128]{2,1,0:T(8,128)S(1)} %get-tuple-element.8), channel_id=1, source_target_pairs={{32,0},{64,32},{96,64},{128,96},{160,128},{192,160},{224,192},{33,... | collective-permute-start | bytes 49160 | tf_op jit(solution)/shard_map/ppermute | solution.py:19
Sparse Core Ops, SparseCore 0:
  12.1 53.0 all-gather.3
  155.5 46.1 all-gather.5
  291.8 46.1 all-gather.7
where the time goes:
time: 436 us; the launch traced here: 435 us
  blocking collectives  227 us (52%)
  waiting for transfers between devices  129 us (30%)
  other arithmetic  21 us (5%)
  matrix products  18.7 us (4%)
  starting transfers between devices  14.2 us (3%)
  between operations  13.4 us (3%)
  local copies, waits for them, and re-layouts  11.6 us (3%)
    psum x3, blocking collectives, local(): gram_sum = lax.psum(partial_value, ('group', 'row'))  227 us
    all_gather x3, waiting for transfers between devices, local(): group_all = lax.all_gather(scaled, 'row', axis=0, tiled=True)  129 us
    dot_general x3, matrix products, local(): jnp.einsum('btij,btkj->bki', tiles, picked, precision=lax.Precision.HIGHE...  15.5 us
    ppermute x3, starting transfers between devices, padded(): before = lax.ppermute(last, axis, up)  10.2 us
  transfers between devices with their start and end apart: 9, of which 3 were waited for; matrix products, arithmetic and copies ran while one was open for 2% of the time, Pallas kernels for 0%

commit v1 on v0

--- a/solution.py
+++ b/solution.py
@@ -53,7 +53,9 @@
     for step_at in range(ITERS):
         scaled = basis * inv_root[:, None, :]
         rimmed = padded(scaled, (("group", 0),), RIM)
-        group_all = lax.all_gather(scaled, "row", axis=0, tiled=True)
+        group_all = jnp.concatenate(
+            lax.all_to_all(jnp.stack([scaled] * lax.axis_size("row")), "row", 0, 0), axis=0
+        )
         received = jnp.take(group_all, gather_pick, axis=0)
         extended = jnp.concatenate([scaled, received, rimmed[:RIM], rimmed[blocks + RIM :]], axis=0)
         picked = jnp.take(extended, tile_cols, axis=0) * live_mask[:, :, None, None]

time: 436 us -> 376 us (0.86)
  waiting for transfers between devices: 129 us -> 69.4 us
  starting transfers between devices: 14.2 us -> 31.2 us
  between operations: 13.4 us -> 0.42 us
    all_gather x3 -> x0, waiting for transfers between devices: 129 us -> none  [local(): group_all = lax.all_gather(scaled, 'row', axis=0, tiled=True)]
    all_to_all x0 -> x3, waiting for transfers between devices: none -> 69.4 us  [local(): lax.all_to_all(jnp.stack([scaled] * lax.axis_size('row')), 'row', 0, 0)]
    all_to_all x0 -> x3, starting transfers between devices: none -> 17.3 us  [local(): lax.all_to_all(jnp.stack([scaled] * lax.axis_size('row')), 'row', 0, 0)]
    another operation x0 -> x3, local copies, waits for them, and re-layouts: none -> 4.77 us  [local(): jnp.stack([scaled] * lax.axis_size('row'))]
    gather x3, local copies, waits for them, and re-layouts: 6.55 us -> 1.89 us  [local(): received = jnp.take(group_all, gather_pick, axis=0)]
  transfers between devices with their start and end apart: 9 -> 9, of which waited for: 3 -> 3; matrix products, arithmetic and copies ran while one was open for 2% -> 1% of each run, Pallas kernels for 0% -> 0%
where the time goes in v1:
time: 376 us; the launch traced here: 375 us
  blocking collectives  229 us (61%)
  waiting for transfers between devices  69.4 us (18%)
  starting transfers between devices  31.2 us (8%)
  other arithmetic  17.9 us (5%)
  matrix products  17.5 us (5%)
  local copies, waits for them, and re-layouts  9.45 us (3%)
    psum x3, blocking collectives, local(): gram_sum = lax.psum(partial_value, ('group', 'row'))  229 us
    all_to_all x3, waiting for transfers between devices, local(): lax.all_to_all(jnp.stack([scaled] * lax.axis_size('row')), 'row', 0, 0)  69.4 us
    all_to_all x3, starting transfers between devices, local(): lax.all_to_all(jnp.stack([scaled] * lax.axis_size('row')), 'row', 0, 0)  17.3 us
    dot_general x3, matrix products, local(): jnp.einsum('btij,btkj->bki', tiles, picked, precision=lax.Precision.HIGHE...  15.5 us
    ppermute x3, starting transfers between devices, padded(): before = lax.ppermute(last, axis, up)  9.86 us
  transfers between devices with their start and end apart: 9, of which 3 were waited for; matrix products, arithmetic and copies ran while one was open for 1% of the time, Pallas kernels for 0%

profile of v1, /device:TPU:1, one launch (start us, length us, event | category | flops | bytes accessed | tf_op | source)
XLA Modules:
  0.0 374.8 jit_solution(9229263293565618943)
XLA Ops:
  0.0 4.5 %multiply_reduce_fusion = f32[8,16,128]{2,1,0:T(8,128)S(1)} fusion(bf16[8,16,128,128]{3,2,1,0:T(8,128)(2,1)} %param.13), kind=kLoop, calls=%fused_computation.6 | loop fusion | flops 6275072 | bytes 4259840 | tf_op jit(solution)/shard_map/btij,bt->bi/reduce_sum | solution.py:45
  4.5 0.0 copy-start.2
  4.5 0.1 fusion.26
  4.6 0.2 fusion.12
  4.8 1.6 stack.14
  6.4 8.6 %all-to-all-start = ((f32[32,8,16,128]{3,2,1,0:T(8,128)}), f32[32,8,16,128]{3,2,1,0:T(8,128)S(1)}, u32[]{:S(2)}, u32[]{:S(2)}) async-start(f32[32,8,16,128]{3,2,1,0:T(8,128)} %stack.14), calls=%async_computation | async-start | bytes 4194304 | tf_op jit(solution)/shard_map/all_to_all | solution.py:57
  15.0 3.5 collective-permute-start
  18.5 1.3 collective-permute-start.1
  19.9 0.1 copy.13
  20.0 0.1 min.12
  20.1 0.1 reshape.132
  20.2 22.6 %all-to-all-done = f32[32,8,16,128]{3,2,1,0:T(8,128)S(1)} async-done(((f32[32,8,16,128]{3,2,1,0:T(8,128)}), f32[32,8,16,128]{3,2,1,0:T(8,128)S(1)}, u32[]{:S(2)}, u32[]{:S(2)}) %all-to-all-start) | async-done | bytes 2097184 | tf_op jit(solution)/shard_map/all_to_all | solution.py:57
  42.8 0.6 gather_fusion
  43.5 0.1 broadcast_select_fusion.2
  43.6 0.0 collective-permute-done.1
  43.7 0.8 gather_fusion.1
  44.4 5.2 %fusion.2 = f32[8,16,128]{2,1,0:T(8,128)S(1)} fusion(bf16[8,16,128,128]{3,2,1,0:T(8,128)(2,1)} %param.13, f32[8,16,16,128]{3,2,1,0:T(8,128)S(1)} %bitcast.95, f32[8,16]{1,0:T(8,128)S(1)} %get-tuple-element.15, pred[8,16]{1,0:T(8,128)(4,1)S(1)} %get-tuple-element.21, f32[8,128]{1,0:T(8,128)S(1)} %add_power_fusion), kind=kOutput, calls=%fused_computation.13 | convolution fusion | flops 403193856 | bytes 5313152 | tf_op jit(solution)/shard_map/btij,btkj->bki/dot_general | solution.py:62
  49.6 0.2 convolution_bitcast_fusion.9
  49.8 79.3 %psum.21 = f32[16,16]{0,1:T(8,128)S(1)} all-reduce(f32[16,16]{0,1:T(8,128)S(1)} %convolution_bitcast_fusion.9), channel_id=1, replica_groups=mesh['group'=8,'row'=32] {'group','row'}, use_global_device_ids=true, to_apply=%region_1.0 | all-reduce | flops 256 | bytes 2048 | tf_op jit(solution)/shard_map/psum | solution.py:71
  129.1 0.1 copy.15
  129.2 1.5 cholesky.59
  130.7 0.6 compare_reduce_fusion.2
  131.3 0.6 fusion.17
  132.0 1.2 custom-call.7
  133.2 0.2 convolution_bitcast_fusion.8
  133.4 0.2 bitcast_multiply_fusion.1
  133.6 1.6 stack.16
  135.2 4.3 %all-to-all-start.1 = ((f32[32,8,16,128]{3,2,1,0:T(8,128)}), f32[32,8,16,128]{3,2,1,0:T(8,128)S(1)}, u32[]{:S(2)}, u32[]{:S(2)}) async-start(f32[32,8,16,128]{3,2,1,0:T(8,128)} %stack.16), calls=%async_computation.1 | async-start | bytes 4194304 | tf_op jit(solution)/shard_map/all_to_all | solution.py:57
  139.6 2.6 collective-permute-start.2
  142.2 1.3 collective-permute-start.3
  143.5 24.0 %all-to-all-done.1 = f32[32,8,16,128]{3,2,1,0:T(8,128)S(1)} async-done(((f32[32,8,16,128]{3,2,1,0:T(8,128)}), f32[32,8,16,128]{3,2,1,0:T(8,128)S(1)}, u32[]{:S(2)}, u32[]{:S(2)}) %all-to-all-start.1) | async-done | bytes 2097184 | tf_op jit(solution)/shard_map/all_to_all | solution.py:57
  167.5 0.6 gather_fusion.2
  168.1 0.1 broadcast_select_fusion.1
  168.3 0.0 collective-permute-done.2
  168.4 0.8 gather_fusion.3
  169.1 5.2 %fusion.1 = f32[8,16,128]{2,1,0:T(8,128)S(1)} fusion(bf16[8,16,128,128]{3,2,1,0:T(8,128)(2,1)} %param.13, f32[8,16,16,128]{3,2,1,0:T(8,128)S(1)} %bitcast.96, f32[8,16]{1,0:T(8,128)S(1)} %get-tuple-element.15, pred[8,16]{1,0:T(8,128)(4,1)S(1)} %get-tuple-element.21, f32[8,128]{1,0:T(8,128)S(1)} %add_power_fusion), kind=kOutput, calls=%fused_computation.11 | convolution fusion | flops 403193856 | bytes 5313152 | tf_op jit(solution)/shard_map/btij,btkj->bki/dot_general | solution.py:62
  174.3 0.2 convolution_bitcast_fusion.7
  174.5 74.4 %psum.22 = f32[16,16]{0,1:T(8,128)S(1)} all-reduce(f32[16,16]{0,1:T(8,128)S(1)} %convolution_bitcast_fusion.7), channel_id=1, replica_groups=mesh['group'=8,'row'=32] {'group','row'}, use_global_device_ids=true, to_apply=%region_4.9 | all-reduce | flops 256 | bytes 2048 | tf_op jit(solution)/shard_map/psum | solution.py:71
  248.9 0.1 copy.17
  249.0 1.5 cholesky.70
  250.5 0.6 compare_reduce_fusion.1
  251.1 0.6 fusion.18
  251.8 1.2 custom-call.8
  253.0 0.2 convolution_bitcast_fusion.6
  253.2 0.2 bitcast_multiply_fusion
  253.4 1.6 stack.18
  255.0 4.3 %all-to-all-start.2 = ((f32[32,8,16,128]{3,2,1,0:T(8,128)}), f32[32,8,16,128]{3,2,1,0:T(8,128)S(1)}, u32[]{:S(2)}, u32[]{:S(2)}) async-start(f32[32,8,16,128]{3,2,1,0:T(8,128)} %stack.18), calls=%async_computation.2 | async-start | bytes 4194304 | tf_op jit(solution)/shard_map/all_to_all | solution.py:57
  259.4 3.7 collective-permute-start.4
  263.0 1.5 collective-permute-start.5
  264.5 22.8 %all-to-all-done.2 = f32[32,8,16,128]{3,2,1,0:T(8,128)S(1)} async-done(((f32[32,8,16,128]{3,2,1,0:T(8,128)}), f32[32,8,16,128]{3,2,1,0:T(8,128)S(1)}, u32[]{:S(2)}, u32[]{:S(2)}) %all-to-all-start.2) | async-done | bytes 2097184 | tf_op jit(solution)/shard_map/all_to_all | solution.py:57
  287.3 0.6 gather_fusion.4
  287.9 0.1 broadcast_select_fusion
  288.1 0.8 gather_fusion.5
  288.9 5.2 %fusion = f32[8,16,128]{2,1,0:T(8,128)S(1)} fusion(bf16[8,16,128,128]{3,2,1,0:T(8,128)(2,1)} %param.13, f32[8,16,16,128]{3,2,1,0:T(8,128)S(1)} %bitcast.94, f32[8,16]{1,0:T(8,128)S(1)} %get-tuple-element.15, pred[8,16]{1,0:T(8,128)(4,1)S(1)} %get-tuple-element.21, f32[8,128]{1,0:T(8,128)S(1)} %add_power_fusion), kind=kOutput, calls=%fused_computation.9 | convolution fusion | flops 403193856 | bytes 5313152 | tf_op jit(solution)/shard_map/btij,btkj->bki/dot_general | solution.py:62
  294.1 0.2 convolution_bitcast_fusion.5
  294.3 75.3 %psum.23 = f32[16,16]{0,1:T(8,128)S(1)} all-reduce(f32[16,16]{0,1:T(8,128)S(1)} %convolution_bitcast_fusion.5), channel_id=1, replica_groups=mesh['group'=8,'row'=32] {'group','row'}, use_global_device_ids=true, to_apply=%region_5.10 | all-reduce | flops 256 | bytes 2048 | tf_op jit(solution)/shard_map/psum | solution.py:71
  369.6 0.1 copy.19
  369.6 1.5 cholesky.81
  371.1 0.6 compare_reduce_fusion
  371.8 0.6 fusion.19
  372.4 1.2 custom-call.9
  373.7 0.2 convolution_bitcast_fusion.4
  373.9 0.2 convolution_bitcast_fusion
  374.1 0.7 pad_maximum_fusion.3
  (34 shorter events, 0.3 us)
Async XLA Ops:
  0.0 4.5 %copy-start.1 = (s32[8,16]{1,0:T(8,128)S(1)}, s32[8,16]{1,0:T(8,128)}, u32[]{:S(2)}) copy-start(s32[8,16]{1,0:T(8,128)} %param.14) | copy-start | bytes 1540
  0.0 4.5 %copy-start.3 = (s32[8]{0:T(128)S(1)}, s32[8]{0:T(128)}, u32[]{:S(2)}) copy-start(s32[8]{0:T(128)} %param.15) | copy-start | bytes 100
  0.0 4.8 %copy-start = (f32[8,16,128]{2,1,0:T(8,128)S(1)}, f32[8,16,128]{2,1,0:T(8,128)}, u32[]{:S(2)}) copy-start(f32[8,16,128]{2,1,0:T(8,128)} %param.12) | copy-start | bytes 196612
  4.5 15.4 %copy-start.2 = (s32[1,1,32,2]{2,3,1,0:T(2,128)S(1)}, s32[1,1,32,2]{2,3,1,0:T(2,128)}, u32[]{:S(2)}) copy-start(s32[1,1,32,2]{2,3,1,0:T(2,128)} %param.16) | copy-start | bytes 772
  6.4 36.4 %all-to-all-start = ((f32[32,8,16,128]{3,2,1,0:T(8,128)}), f32[32,8,16,128]{3,2,1,0:T(8,128)S(1)}, u32[]{:S(2)}, u32[]{:S(2)}) async-start(f32[32,8,16,128]{3,2,1,0:T(8,128)} %stack.14), calls=%async_computation | async-start | bytes 4194304 | tf_op jit(solution)/shard_map/all_to_all | solution.py:57
  15.0 28.6 %collective-permute-start = (f32[2,16,128]{2,1,0:T(8,128)S(1)}, f32[2,16,128]{2,1,0:T(8,128)S(1)}, u32[]{:S(2)}, u32[]{:S(2)}) collective-permute-start(f32[2,16,128]{2,1,0:T(8,128)S(1)} %get-tuple-element.13), channel_id=1, source_target_pairs={{0,32},{32,64},{64,96},{96,128},{128,160},{160,192},{192,224},{1,3... | collective-permute-start | bytes 49160 | tf_op jit(solution)/shard_map/ppermute | solution.py:18
  18.5 25.1 %collective-permute-start.1 = (f32[2,16,128]{2,1,0:T(8,128)S(1)}, f32[2,16,128]{2,1,0:T(8,128)S(1)}, u32[]{:S(2)}, u32[]{:S(2)}) collective-permute-start(f32[2,16,128]{2,1,0:T(8,128)S(1)} %get-tuple-element.14), channel_id=1, source_target_pairs={{32,0},{64,32},{96,64},{128,96},{160,128},{192,160},{224,192},{33,... | collective-permute-start | bytes 49160 | tf_op jit(solution)/shard_map/ppermute | solution.py:19
  135.2 32.3 %all-to-all-start.1 = ((f32[32,8,16,128]{3,2,1,0:T(8,128)}), f32[32,8,16,128]{3,2,1,0:T(8,128)S(1)}, u32[]{:S(2)}, u32[]{:S(2)}) async-start(f32[32,8,16,128]{3,2,1,0:T(8,128)} %stack.16), calls=%async_computation.1 | async-start | bytes 4194304 | tf_op jit(solution)/shard_map/all_to_all | solution.py:57
  139.6 28.7 %collective-permute-start.2 = (f32[2,16,128]{2,1,0:T(8,128)S(1)}, f32[2,16,128]{2,1,0:T(8,128)S(1)}, u32[]{:S(2)}, u32[]{:S(2)}) collective-permute-start(f32[2,16,128]{2,1,0:T(8,128)S(1)} %get-tuple-element.10), channel_id=1, source_target_pairs={{0,32},{32,64},{64,96},{96,128},{128,160},{160,192},{192,224},{1,3... | collective-permute-start | bytes 49160 | tf_op jit(solution)/shard_map/ppermute | solution.py:18
  142.2 26.1 %collective-permute-start.3 = (f32[2,16,128]{2,1,0:T(8,128)S(1)}, f32[2,16,128]{2,1,0:T(8,128)S(1)}, u32[]{:S(2)}, u32[]{:S(2)}) collective-permute-start(f32[2,16,128]{2,1,0:T(8,128)S(1)} %get-tuple-element.12), channel_id=1, source_target_pairs={{32,0},{64,32},{96,64},{128,96},{160,128},{192,160},{224,192},{33,... | collective-permute-start | bytes 49160 | tf_op jit(solution)/shard_map/ppermute | solution.py:19
  255.0 32.3 %all-to-all-start.2 = ((f32[32,8,16,128]{3,2,1,0:T(8,128)}), f32[32,8,16,128]{3,2,1,0:T(8,128)S(1)}, u32[]{:S(2)}, u32[]{:S(2)}) async-start(f32[32,8,16,128]{3,2,1,0:T(8,128)} %stack.18), calls=%async_computation.2 | async-start | bytes 4194304 | tf_op jit(solution)/shard_map/all_to_all | solution.py:57
  259.4 28.7 %collective-permute-start.4 = (f32[2,16,128]{2,1,0:T(8,128)S(1)}, f32[2,16,128]{2,1,0:T(8,128)S(1)}, u32[]{:S(2)}, u32[]{:S(2)}) collective-permute-start(f32[2,16,128]{2,1,0:T(8,128)S(1)} %get-tuple-element.6), channel_id=1, source_target_pairs={{0,32},{32,64},{64,96},{96,128},{128,160},{160,192},{192,224},{1,3... | collective-permute-start | bytes 49160 | tf_op jit(solution)/shard_map/ppermute | solution.py:18
  263.0 25.0 %collective-permute-start.5 = (f32[2,16,128]{2,1,0:T(8,128)S(1)}, f32[2,16,128]{2,1,0:T(8,128)S(1)}, u32[]{:S(2)}, u32[]{:S(2)}) collective-permute-start(f32[2,16,128]{2,1,0:T(8,128)S(1)} %get-tuple-element.8), channel_id=1, source_target_pairs={{32,0},{64,32},{96,64},{128,96},{160,128},{192,160},{224,192},{33,... | collective-permute-start | bytes 49160 | tf_op jit(solution)/shard_map/ppermute | solution.py:19
